TPU v7x, 128 devices: a whole 4x4x4 slice. The times are simulated.
128 devices in a mesh: row: 16 (over z, y_hi, core), col: 4 (over x), depth: 2 (over y_lo).
Axes of the slice: x: 4, y: 4 (y_hi: 2, y_lo: 2; y = y_hi * 2 + y_lo), z: 4, core: 2. Of those that a mesh axis runs over, the one named last changes fastest.
Arguments:
- left_block: bfloat16 [4, 32768, 512], P(None, ('row', 'depth'), 'col'), may hold values from -6 to 6
- right_block: bfloat16 [512, 2, 16384], P(('row', 'depth'), None, 'col'), may hold values from -0.125 to 0.125
- slice_ids: int32 [4], replicated, may hold values from 0 to 1, as said below
- mode_order: int32 [9], replicated, may hold values from 0 to 8, each once
Outputs:
- contracted: float32 [32768, 16384], P(('row', 'depth'), 'col')
Inputs may be any that keep to these rules, and one draw needn't show every extreme that they name: mode_order holds every number of 0 to 8 once. `slice_ids`: each value of the sliced bond is taken by exactly 2 slices.
All inputs are finite; a program needn't handle non-finite values.
Results may differ from a plain program's by a relative error of at most 0.0003.
Values may be sent and summed in bfloat16 or wider, within the bound.
A program may use at most 128 MiB of HBM per device.

v0:
```python
import jax
import jax.numpy as jnp
from jax import lax
from jax.sharding import PartitionSpec as P


def stored_order(mode_order, columns):
    logical = jnp.arange(columns, dtype=jnp.int32)
    stored = jnp.zeros((columns,), jnp.int32)
    for bit_place in range(mode_order.shape[0]):
        stored = stored + logical // 2**bit_place % 2 * jnp.left_shift(
            jnp.int32(1), mode_order[bit_place]
        )
    return stored


def per_device(left_block, right_block, slice_ids, mode_order):
    values = right_block.shape[1]
    picks = (slice_ids[:, None] == jnp.arange(values, dtype=jnp.int32)[None, :]).astype(jnp.float32)
    folded = jnp.zeros((values,) + left_block.shape[1:], jnp.float32)
    for number in range(left_block.shape[0]):
        folded = (
            folded + picks[number][:, None, None] * left_block[number].astype(jnp.float32)[None]
        )
    whole_left = lax.all_gather(folded, "col", axis=2, tiled=True)
    permuted = jnp.take(whole_left, stored_order(mode_order, whole_left.shape[2]), axis=2)
    return jnp.einsum(
        "crk,kcn->rn",
        permuted,
        lax.all_gather(right_block, ("row", "depth"), axis=0, tiled=True).astype(jnp.float32),
        preferred_element_type=jnp.float32,
        precision=lax.Precision.HIGHEST,
    )


def solution(mesh):
    in_specs = (P(None, ("row", "depth"), "col"), P(("row", "depth"), None, "col"), P(), P())
    out_specs = P(("row", "depth"), "col")
    return jax.shard_map(
        per_device, mesh=mesh, in_specs=in_specs, out_specs=out_specs, check_vma=False
    )
```

profile of v0, /device:TPU:1, one launch (start us, length us, event | category | flops | bytes accessed | tf_op | source)
XLA Modules:
  0.0 200.5 jit_solution(12950660524431879594)
XLA Ops:
  6.5 0.0 all-gather.3.cloned.1.call-start
  6.5 0.7 fusion.70
  7.3 1.3 bitcast_convert_fusion.3
  8.6 0.0 copy-start
  8.6 0.2 copy.12
  8.8 0.0 copy-start.1
  8.8 0.2 copy.13
  9.0 0.2 copy.15
  9.2 0.2 copy.14
  9.4 1.9 multiply_add_fusion
  11.3 0.0 all-gather.3.cloned.1.call-update
  11.4 0.0 all-gather.5.cloned.1.call-start
  11.4 0.0 copy-done
  11.4 0.8 copy.16
  12.3 0.0 all-gather.5.cloned.1.call-update
  12.3 0.0 copy-done.1
  12.3 0.7 fusion.71
  18.7 44.3 %all-gather.3.cloned.1.call-done = f32[2,1024,512]{1,0,2:T(2,128)} async-done(((f32[2,1024,128]{1,0,2:T(2,128)}), f32[2,1024,512]{1,0,2:T(2,128)}) %all-gather.3.cloned.1.call-update) | async-done | bytes 4194320 | tf_op jit(solution)/shard_map/all_gather | solution.py:25
  63.0 21.9 %gather_fusion = f32[512,2,1024]{2,1,0:T(2,128)} fusion(f32[2,1024,512]{1,0,2:T(2,128)} %all-gather.3.cloned.1.call-done, s32[1024]{0:T(1024)S(1)} %pad_clamp_fusion), kind=kCustom, calls=%fused_computation | custom fusion | bytes 8390656 | tf_op jit(solution)/shard_map/jit(_take)/gather | solution.py:26
  84.9 6.0 %select_bitcast_fusion = f32[2,1024,512]{1,0,2:T(2,128)} fusion(f32[512,2,1024]{2,1,0:T(2,128)} %gather_fusion, pred[512]{0:T(512)(128)(4,1)S(1)} %compare_and_fusion), kind=kLoop, calls=%fused_computation.3 | loop fusion | flops 1048576 | bytes 8389120 | tf_op jit(solution)/shard_map/jit(_take)/select_n | solution.py:26
  90.9 67.0 %all-gather.5.cloned.1.call-done = bf16[512,2,4096]{2,0,1:T(8,128)(2,1)} async-done(((bf16[16,2,4096]{2,0,1:T(8,128)(2,1)}), bf16[512,2,4096]{2,0,1:T(8,128)(2,1)}) %all-gather.5.cloned.1.call-update) | async-done | bytes 8388624 | tf_op jit(solution)/shard_map/all_gather | solution.py:30
  157.9 35.8 %convolution_bitcast_fusion = f32[1024,4096]{1,0:T(8,128)} fusion(bf16[512,2,4096]{2,0,1:T(8,128)(2,1)} %all-gather.5.cloned.1.call-done, f32[2,1024,512]{1,0,2:T(2,128)} %select_bitcast_fusion), kind=kOutput, calls=%fused_computation.1 | convolution fusion | flops 51539607552 | bytes 29360128 | tf_op jit(solution)/shard_map/crk,kcn->rn/dot_general | solution.py:27
  (4 shorter events, 0.1 us)
Async XLA Ops:
  6.5 56.4 %all-gather.3.cloned.1.call-start = ((), (), s32[]{:S(2)}) async-start(), calls=%async_computation | async-start | bytes 5242880 | tf_op jit(solution)/shard_map/all_gather | solution.py:25
  8.6 2.8 %copy-start = (bf16[16,2,4096]{2,1,0:T(2,128)(2,1)S(1)}, bf16[16,2,4096]{2,1,0:T(2,128)(2,1)}, u32[]{:S(2)}) copy-start(bf16[16,2,4096]{2,1,0:T(2,128)(2,1)} %param.5) | copy-start | bytes 786436
  8.8 3.5 %copy-start.1 = (s32[9]{0:T(128)S(1)}, s32[9]{0:T(128)}, u32[]{:S(2)}) copy-start(s32[9]{0:T(128)} %param.7) | copy-start | bytes 112
  11.4 146.5 %all-gather.5.cloned.1.call-start = ((), (), s32[]{:S(2)}) async-start(), calls=%async_computation.1 | async-start | bytes 8650752 | tf_op jit(solution)/shard_map/all_gather | solution.py:30
Sparse Core Ops, SparseCore 0:
  11.5 51.4 all-gather.2
  64.6 93.1 all-gather.4
where the time goes:
time: 201 us; the launch traced here: 200 us
  waiting for transfers between devices  111 us (55%)
  matrix products  35.8 us (18%)
  local copies, waits for them, and re-layouts  24.2 us (12%)
  between operations  19.1 us (10%)
  other arithmetic  10 us (5%)
    all_gather x1, waiting for transfers between devices, per_device(): lax.all_gather(right_block, ('row', 'depth'), axis=0, tiled=True)  67 us
    all_gather x1, waiting for transfers between devices, per_device(): whole_left = lax.all_gather(folded, 'col', axis=2, tiled=True)  44.3 us
    dot_general x1, matrix products, per_device(): jnp.einsum('crk,kcn->rn', permuted, lax.all_gather(right_block, ('row', '...  35.8 us
    gather x1, local copies, waits for them, and re-layouts, per_device(): jnp.take(whole_left, stored_order(mode_order, whole_left.shape[2]), axis=2)  21.9 us
    select_n x2, other arithmetic, per_device(): jnp.take(whole_left, stored_order(mode_order, whole_left.shape[2]), axis=2)  6.05 us
  transfers between devices with their start and end apart: 2, of which 2 were waited for; matrix products, arithmetic and copies ran while one was open for 15% of the time, Pallas kernels for 0%

commit v1 on v0

v1 whole, which is shorter than its diff:
```python
import functools
import math

import jax
import jax.numpy as jnp
import numpy as np
from jax import lax
from jax.experimental import pallas as pl
from jax.experimental.pallas import tpu as pltpu
from jax.sharding import PartitionSpec as P

MESH = pl.DeviceIdType.MESH
CHUNKS = 8
EARLY = 7
CODE_TOP = 32000.0
STEPS_PER_OCTAVE = 16.0
LN2 = math.log(2.0)


def tile_product(a_ref, b_ref, i, j, width):
    cols = pl.ds(pl.multiple_of(j * width, width), width)
    b = b_ref[:, :, :, :, :, cols]
    b = b.reshape(-1, width)
    both = jnp.dot(a_ref[i], b, preferred_element_type=jnp.float32)
    rows = both.shape[0] // 2
    return both[:rows] + both[rows:]


def gather_kernel(
    ids_ref,
    order_ref,
    left_ref,
    right_ref,
    a_ref,
    b_ref,
    part_ref,
    code,
    pick,
    send1,
    recv1,
    send,
    recv,
):
    slices, rows_all, part_k = left_ref.shape
    values, shard_k, columns = right_ref.shape
    rows, width = rows_all // CHUNKS, columns // CHUNKS
    bond = 4 * part_k

    row, c, y_lo = lax.axis_index("row"), lax.axis_index("col"), lax.axis_index("depth")
    core = row % 2
    y = (row // 2) % 2 * 2 + y_lo
    z = row // 4
    p1 = y * (1 - core) + z * core
    p2 = z * (1 - core) + y * core

    def place(y_at, z_at, core_at):
        return ((z_at * 2 + y_at // 2) * 2 + core_at, c, y_at % 2)

    def first(d):
        return place((y + (1 - core) * d) % 4, (z + core * d) % 4, core)

    def second(d):
        return place((y + core * d) % 4, (z + (1 - core) * d) % 4, core)

    def along(d):
        return (row, (c + d) % 4, y_lo)

    sibling = place(y, z, 1 - core)

    barrier = pltpu.get_barrier_semaphore()
    for other in (first(1), first(3), second(1), second(3), along(1), along(3), sibling):
        pl.semaphore_signal(barrier, inc=1, device_id=other, device_id_type=MESH)

    own = b_ref.at[:, core, p2, p1]
    own[...] = right_ref[...]

    def copy(ref, sems, at, device):
        return pltpu.make_async_remote_copy(
            src_ref=ref,
            dst_ref=ref,
            send_sem=sems[0].at[at],
            recv_sem=sems[1].at[at],
            device_id=device,
            device_id_type=MESH,
        )

    once, many = (send1, recv1), (send, recv)
    left1, right1, far1 = (p1 + 3) % 4, (p1 + 1) % 4, (p1 + 2) % 4

    def phase1(kind):
        if kind == 0:
            return copy(own, once, 0, first(1)), b_ref.at[:, core, p2, left1]
        if kind == 1:
            return copy(own, once, 1, first(3)), b_ref.at[:, core, p2, right1]
        if kind == 2:
            return copy(b_ref.at[0, core, p2, left1], once, 2, first(1)), b_ref.at[0, core, p2, far1]
        return copy(b_ref.at[1, core, p2, right1], once, 3, first(3)), b_ref.at[1, core, p2, far1]

    def start1(kind):
        phase1(kind)[0].start()

    def arrived1(kind):
        copy(phase1(kind)[1], once, kind, sibling).wait_recv()

    def sent1(kind):
        phase1(kind)[0].wait_send()

    left2, right2, far2 = (p2 + 3) % 4, (p2 + 1) % 4, (p2 + 2) % 4

    def moved(kind, t):
        cols = pl.ds(pl.multiple_of(t * width, width), width)

        def group(plane, p):
            return b_ref.at[:, plane, p, :, :, cols]

        def half(v, p):
            return b_ref.at[v, core, p, :, :, cols]

        if kind == 0:
            return group(core, p2), second(1), group(core, left2)
        if kind == 1:
            return group(core, p2), second(3), group(core, right2)
        if kind == 2:
            return half(0, left2), second(1), half(0, far2)
        if kind == 3:
            return half(1, right2), second(3), half(1, far2)
        if kind == 4:
            return group(core, p2), sibling, group(1 - core, p1)
        if kind == 5:
            return group(core, left2), sibling, group(1 - core, left1)
        if kind == 6:
            return group(core, right2), sibling, group(1 - core, right1)
        if kind == 7:
            return group(core, far2), sibling, group(1 - core, far1)
        if kind == 8:
            return code.at[t, c], along(1), code.at[t, (c + 3) % 4]
        if kind == 9:
            return code.at[t, c], along(3), code.at[t, (c + 1) % 4]
        if kind == 10:
            return code.at[t, (c + 3) % 4, 0], along(1), code.at[t, (c + 2) % 4, 0]
        return code.at[t, (c + 1) % 4, 1], along(3), code.at[t, (c + 2) % 4, 1]

    def start(kind, t):
        ref, device, _ = moved(kind, t)
        copy(ref, many, (kind, t), device).start()

    def arrived(kind, t):
        copy(moved(kind, t)[2], many, (kind, t), sibling).wait_recv()

    def sent(kind, t):
        ref, device, _ = moved(kind, t)
        copy(ref, many, (kind, t), device).wait_send()

    pl.semaphore_wait(barrier, 7)
    start1(0)
    start1(1)

    weights = [
        [jnp.where(ids_ref[s] == v, 1.0, 0.0).astype(jnp.float32) for s in range(slices)]
        for v in range(values)
    ]

    def encode(t, carry):
        here = pl.ds(pl.multiple_of(t * rows, rows), rows)
        blocks = [left_ref[s, here, :].astype(jnp.float32) for s in range(slices)]
        for v in range(values):
            total = blocks[0] * weights[v][0]
            for s in range(1, slices):
                total = total + blocks[s] * weights[v][s]
            top = jnp.max(jnp.abs(total), axis=0, keepdims=True)
            top = jnp.maximum(top, 2.0**-110)
            level = jnp.ceil(jnp.log(top) * (STEPS_PER_OCTAVE / LN2))
            scale = jnp.exp(level * (-LN2 / STEPS_PER_OCTAVE)) * CODE_TOP
            code[t, c, v, :rows, :] = jnp.round(total * scale).astype(jnp.int32).astype(jnp.int16)
            code[t, c, v, rows:, :] = jnp.broadcast_to(level, (16, part_k)).astype(jnp.int32).astype(jnp.int16)
        start(8, t)
        start(9, t)
        return carry

    lax.fori_loop(0, CHUNKS, encode, 0)

    place_at = lax.broadcasted_iota(jnp.int32, (bond, bond), 1)
    j = place_at & 15
    q1, q2, plane = (place_at >> 4) & 3, (place_at >> 6) & 3, place_at >> 8
    at_y = q1 * (1 - plane) + q2 * plane
    at_z = q2 * (1 - plane) + q1 * plane
    shard = at_z * 8 + (at_y >> 1) * 4 + plane * 2 + (at_y & 1)
    logical = shard * shard_k + j
    stored = jnp.zeros((bond, bond), jnp.int32)
    for bit in range(order_ref.shape[0]):
        stored = stored + ((logical >> bit) & 1) * jnp.left_shift(jnp.int32(1), order_ref[bit])
    hit = lax.broadcasted_iota(jnp.int32, (bond, bond), 0) == stored
    pick[...] = jnp.where(hit, 1.0, 0.0).astype(jnp.bfloat16)

    arrived1(0)
    start1(2)
    arrived1(1)
    start1(3)
    arrived1(2)
    arrived1(3)

    def lead(t):
        for kind in (0, 1, 4):
            start(kind, t)

    lead(0)
    lead(1)

    def decode(t):
        parts = []
        for v in range(values):
            high, low = [], []
            for at in range(4):
                level = code[t, at, v, rows:, :].astype(jnp.int32).astype(jnp.float32)[:1]
                scale = jnp.exp(level * (LN2 / STEPS_PER_OCTAVE)) * (1.0 / CODE_TOP)
                x = code[t, at, v, :rows, :].astype(jnp.int32).astype(jnp.float32) * scale
                h = x.astype(jnp.bfloat16)
                high.append(h)
                low.append((x - h.astype(jnp.float32)).astype(jnp.bfloat16))
            parts += [jnp.concatenate(high, axis=1), jnp.concatenate(low, axis=1)]
        picked = jnp.dot(
            jnp.concatenate(parts, axis=0), pick[...], preferred_element_type=jnp.float32
        ).astype(jnp.bfloat16)
        for v in range(values):
            a_ref[t, :, v * bond : (v + 1) * bond] = picked[2 * rows * v : 2 * rows * (v + 1)]

    def tile(i, j):
        here = pl.ds(pl.multiple_of(i * rows, rows), rows)
        cols = pl.ds(pl.multiple_of(j * width, width), width)
        part_ref[here, cols] = tile_product(a_ref, b_ref, i, j, width)

    def tick(t, carry):
        @pl.when(t < CHUNKS)
        def _():
            arrived(8, t)
            start(10, t)
            arrived(9, t)
            start(11, t)
            arrived(0, t)
            start(2, t)
            start(5, t)
            arrived(1, t)
            start(3, t)
            start(6, t)

        @pl.when(t < CHUNKS - 2)
        def _():
            lead(t + 2)

        @pl.when((t >= 1) & (t < CHUNKS + 1))
        def _():
            arrived(2, t - 1)
            arrived(3, t - 1)
            start(7, t - 1)
            arrived(10, t - 1)
            arrived(11, t - 1)
            decode(t - 1)

        @pl.when(t >= 2)
        def _():
            for kind in (4, 5, 6, 7):
                arrived(kind, t - 2)

        @pl.when((t >= 2) & (t < EARLY + 2))
        def _():
            u = t - 2

            def across(q, carry):
                tile(u, q)
                return carry

            def down(q, carry):
                tile(q, u)
                return carry

            lax.fori_loop(0, u, across, 0)
            lax.fori_loop(0, u + 1, down, 0)

        return carry

    lax.fori_loop(0, CHUNKS + 2, tick, 0)

    for kind in range(4):
        sent1(kind)

    def settle(t, carry):
        for kind in range(12):
            sent(kind, t)
        return carry

    lax.fori_loop(0, CHUNKS, settle, 0)


def finish_kernel(a_ref, b_ref, part_ref, out_ref, last, sems):
    rows, width = last.shape[1], last.shape[2]
    early = part_ref.shape
    done = pltpu.make_async_copy(
        part_ref, out_ref.at[: early[0], : early[1]], sems.at[2 * CHUNKS - 1]
    )
    done.start()
    u = CHUNKS - 1

    def out_copy(q, i, j):
        here = pl.ds(pl.multiple_of(i * rows, rows), rows)
        cols = pl.ds(pl.multiple_of(j * width, width), width)
        return pltpu.make_async_copy(last.at[q], out_ref.at[here, cols], sems.at[q])

    def across(q, carry):
        last[q] = tile_product(a_ref, b_ref, u, q, width)
        out_copy(q, u, q).start()
        return carry

    def down(q, carry):
        last[u + q] = tile_product(a_ref, b_ref, q, u, width)
        out_copy(u + q, q, u).start()
        return carry

    lax.fori_loop(0, u, across, 0)
    lax.fori_loop(0, u + 1, down, 0)

    def across_wait(q, carry):
        out_copy(q, u, q).wait()
        return carry

    def down_wait(q, carry):
        out_copy(u + q, q, u).wait()
        return carry

    lax.fori_loop(0, u, across_wait, 0)
    lax.fori_loop(0, u + 1, down_wait, 0)
    done.wait()


def per_device(left_block, right_block, slice_ids, mode_order):
    slices, rows_all, part_k = left_block.shape
    shard_k, values, columns = right_block.shape
    rows, width = rows_all // CHUNKS, columns // CHUNKS
    bond = 4 * part_k
    right = jnp.transpose(right_block, (1, 0, 2))
    vmem = pl.BlockSpec(memory_space=pltpu.VMEM)
    smem = pl.BlockSpec(memory_space=pltpu.SMEM)
    a, b, part = pl.pallas_call(
        gather_kernel,
        out_shape=(
            pltpu.VMEM((CHUNKS, 2 * rows, values * bond), jnp.bfloat16),
            pltpu.VMEM((values, 2, 4, 4, shard_k, columns), jnp.bfloat16),
            pltpu.VMEM((EARLY * rows, EARLY * width), jnp.float32),
        ),
        in_specs=[smem, smem, vmem, vmem],
        out_specs=(vmem, vmem, vmem),
        scratch_shapes=[
            pltpu.VMEM((CHUNKS, 4, values, rows + 16, part_k), jnp.int16),
            pltpu.VMEM((bond, bond), jnp.bfloat16),
            pltpu.SemaphoreType.DMA((4,)),
            pltpu.SemaphoreType.DMA((4,)),
            pltpu.SemaphoreType.DMA((12, CHUNKS)),
            pltpu.SemaphoreType.DMA((12, CHUNKS)),
        ],
        compiler_params=pltpu.CompilerParams(
            collective_id=0, has_side_effects=True, vmem_limit_bytes=16 << 20
        ),
    )(slice_ids, mode_order, left_block, right)
    return pl.pallas_call(
        finish_kernel,
        out_shape=jax.ShapeDtypeStruct((rows_all, columns), jnp.float32),
        in_specs=[vmem, vmem, vmem],
        out_specs=pl.BlockSpec(memory_space=pl.ANY),
        scratch_shapes=[
            pltpu.VMEM((2 * CHUNKS - 1, rows, width), jnp.float32),
            pltpu.SemaphoreType.DMA((2 * CHUNKS,)),
        ],
        compiler_params=pltpu.CompilerParams(vmem_limit_bytes=16 << 20),
    )(a, b, part)


def solution(mesh):
    in_specs = (P(None, ("row", "depth"), "col"), P(("row", "depth"), None, "col"), P(), P())
    out_specs = P(("row", "depth"), "col")
    return jax.shard_map(
        per_device, mesh=mesh, in_specs=in_specs, out_specs=out_specs, check_vma=False
    )
```

time: 201 us -> 69.1 us (0.34)
  waiting for transfers between devices: 111 us -> 0 us
  Pallas kernels: 0 us -> 64.6 us
  matrix products: 35.8 us -> 0 us
  local copies, waits for them, and re-layouts: 24.2 us -> 3.63 us
  between operations: 19.1 us -> 0.02 us
  other arithmetic: 10 us -> 0 us
    all_gather x2 -> x0, waiting for transfers between devices: 111 us -> none  [the longest x1 67 us: per_device(): lax.all_gather(right_block, ('row', 'depth'), axis=0, tiled=True)]
    pallas_call x0 -> x2, Pallas kernels: none -> 64.6 us  [the longest x1 57.1 us: per_device(): pl.pallas_call(gather_kernel, out_shape=(pltpu.VMEM((CHUNKS, 2 * rows, va...]
    dot_general x1 -> x0, matrix products: 35.8 us -> none  [per_device(): jnp.einsum('crk,kcn->rn', permuted, lax.all_gather(right_block, ('row', '...]
    gather x1 -> x0, local copies, waits for them, and re-layouts: 21.9 us -> none  [per_device(): jnp.take(whole_left, stored_order(mode_order, whole_left.shape[2]), axis=2)]
    select_n x2 -> x0, other arithmetic: 6.05 us -> none  [per_device(): jnp.take(whole_left, stored_order(mode_order, whole_left.shape[2]), axis=2)]
    unnamed x5 -> x7, local copies, waits for them, and re-layouts: 0.86 us -> 3.63 us
  transfers between devices with their start and end apart: 2 -> 0, of which waited for: 2 -> 0; matrix products, arithmetic and copies ran while one was open for 15% -> 0% of each run, Pallas kernels for 0% -> 0%
where the time goes in v1:
time: 69.1 us; the launch traced here: 68.3 us
  Pallas kernels  64.6 us (93%)
  local copies, waits for them, and re-layouts  3.63 us (5%)
    pallas_call x1, Pallas kernels, per_device(): pl.pallas_call(gather_kernel, out_shape=(pltpu.VMEM((CHUNKS, 2 * rows, va...  57.1 us
    pallas_call x1, Pallas kernels, per_device(): pl.pallas_call(finish_kernel, out_shape=jax.ShapeDtypeStruct((rows_all, c...  7.5 us
    unnamed x7, local copies, waits for them, and re-layouts  3.63 us

profile of v1, /device:TPU:1, one launch (start us, length us, event | category | flops | bytes accessed | tf_op | source)
XLA Modules:
  0.0 68.3 jit_solution(12791708519107720245)
XLA Ops:
  0.0 1.1 %copy.7 = bf16[16,2,4096]{2,0,1:T(8,128)(2,1)S(1)} copy(bf16[16,2,4096]{2,1,0:T(2,128)(2,1)} %param.5) | data formatting | bytes 524288 | tf_op args[1]
  1.1 0.0 copy-start
  1.1 1.2 %copy-done = bf16[4,1024,128]{2,1,0:T(8,128)(2,1)S(1)} copy-done((bf16[4,1024,128]{2,1,0:T(8,128)(2,1)S(1)}, bf16[4,1024,128]{2,1,0:T(8,128)(2,1)}, u32[]{:S(2)}) %copy-start) | copy-done | bytes 1048600
  2.3 0.0 copy-start.1
  2.3 0.7 copy-done.1
  3.0 0.0 copy-start.2
  3.0 0.7 copy-done.2
  3.6 57.1 %shard_map.46 = (bf16[8,256,1024]{2,1,0:T(8,128)(2,1)S(1)}, bf16[2,2,4,4,16,4096]{5,4,3,2,1,0:T(8,128)(2,1)S(1)}, f32[896,3584]{1,0:T(8,128)S(1)}) custom-call(s32[4]{0:T(128)S(1)} %copy-done.1, s32[9]{0:T(128)S(1)} %copy-done.2, bf16[4,1024,128]{2,1,0:T(8,128)(2,1)S(1)} %copy-done, bf16[2,16,4096]{2,1,0:T(8,128)(2,1)S(1)} %bitcast.3), custom_call_target="tpu_custom_call" | custom-call | tf_op jit(solution)/shard_map/pallas_call | solution.py:342
  60.8 7.5 %shard_map.47 = f32[1024,4096]{1,0:T(8,128)} custom-call(bf16[8,256,1024]{2,1,0:T(8,128)(2,1)S(1)} %get-tuple-element.8.a_ref, bf16[2,2,4,4,16,4096]{5,4,3,2,1,0:T(8,128)(2,1)S(1)} %get-tuple-element.9.b_ref, f32[896,3584]{1,0:T(8,128)S(1)} %get-tuple-element.10.part_ref), custom_call_target="tpu_custom_call" | custom-call | tf_op jit(solution)/shard_map/pallas_call | solution.py:363
Async XLA Ops:
  1.1 1.2 %copy-start = (bf16[4,1024,128]{2,1,0:T(8,128)(2,1)S(1)}, bf16[4,1024,128]{2,1,0:T(8,128)(2,1)}, u32[]{:S(2)}) copy-start(bf16[4,1024,128]{2,1,0:T(8,128)(2,1)} %left_ref.1) | copy-start | bytes 3145732
  2.3 0.7 copy-start.1
  3.0 0.7 copy-start.2

commit v2 on v0

v2 whole, which is shorter than its diff:
```python
import functools
import math

import jax
import jax.numpy as jnp
from jax import lax
from jax.experimental import pallas as pl
from jax.experimental.pallas import tpu as pltpu
from jax.sharding import PartitionSpec as P

MESH = pl.DeviceIdType.MESH
ROW_CHUNKS = 4
PAIRS = 4
EARLY = 3
CODE_TOP = 32000.0
STEPS_PER_OCTAVE = 16.0
LN2 = math.log(2.0)


def tile_product(a_ref, b_ref, i, j, width):
    cols = pl.ds(pl.multiple_of(j * width, width), width)
    b = b_ref[:, :, :, :, :, cols]
    b = b.reshape(-1, width)
    both = jnp.dot(a_ref[i], b, preferred_element_type=jnp.float32)
    rows = both.shape[0] // 2
    return both[:rows] + both[rows:]


def gather_kernel(
    ids_hbm,
    order_hbm,
    left_hbm,
    right_ref,
    a_ref,
    b_ref,
    part_ref,
    ids,
    order,
    left,
    code,
    pick,
    local,
    send,
    recv,
    left_send,
    left_recv,
):
    slices, rows_all, part_k = left.shape
    values, shard_k, columns = right_ref.shape
    rows, width = rows_all // ROW_CHUNKS, columns // PAIRS
    strip = width // 2
    bond = 4 * part_k

    row, c, y_lo = lax.axis_index("row"), lax.axis_index("col"), lax.axis_index("depth")
    core = row % 2
    y = (row // 2) % 2 * 2 + y_lo
    z = row // 4

    def place(y_at, z_at, core_at):
        return ((z_at * 2 + y_at // 2) * 2 + core_at, c, y_at % 2)

    def along_y(d):
        return place((y + d) % 4, z, core)

    def along_z(d):
        return place(y, (z + d) % 4, core)

    def along_x(d):
        return (row, (c + d) % 4, y_lo)

    sibling = place(y, z, 1 - core)

    barrier = pltpu.get_barrier_semaphore()
    for other in (along_y(1), along_y(3), along_z(1), along_z(3), along_x(1), along_x(3), sibling):
        pl.semaphore_signal(barrier, inc=1, device_id=other, device_id_type=MESH)

    staged = [
        pltpu.make_async_copy(left_hbm, left, local.at[0]),
        pltpu.make_async_copy(ids_hbm, ids, local.at[1]),
        pltpu.make_async_copy(order_hbm, order, local.at[2]),
    ]
    for one in staged:
        one.start()
    b_ref[:, core, z, y] = right_ref[...]

    def copy(ref, sems, at, device):
        return pltpu.make_async_remote_copy(
            src_ref=ref,
            dst_ref=ref,
            send_sem=sems[0].at[at],
            recv_sem=sems[1].at[at],
            device_id=device,
            device_id_type=MESH,
        )

    many, lefts = (send, recv), (left_send, left_recv)

    def moved(half, kind, p):
        cols = pl.ds(pl.multiple_of(p * width + half * strip, strip), strip)
        first, second = (along_y, along_z) if half == 0 else (along_z, along_y)
        at1, at2 = (y, z) if half == 0 else (z, y)

        def one(v, d):
            at = (at1 + d) % 4
            where = (z, at) if half == 0 else (at, y)
            return b_ref.at[(v, core, *where, slice(None), cols)]

        def group(v, plane, d):
            at = (at2 + d) % 4
            where = (at, slice(None)) if half == 0 else (slice(None), at)
            return b_ref.at[(v, plane, *where, slice(None), cols)]

        both = slice(None)
        if kind == 0:
            return one(both, 0), first(1), one(both, 3)
        if kind == 1:
            return one(both, 0), first(3), one(both, 1)
        if kind == 2:
            return one(0, 3), first(1), one(0, 2)
        if kind == 3:
            return one(1, 1), first(3), one(1, 2)
        if kind == 4:
            return group(both, core, 0), second(1), group(both, core, 3)
        if kind == 5:
            return group(both, core, 0), second(3), group(both, core, 1)
        if kind == 6:
            return group(0, core, 3), second(1), group(0, core, 2)
        if kind == 7:
            return group(1, core, 1), second(3), group(1, core, 2)
        d = (0, 3, 1, 2)[kind - 8]
        return group(both, core, d), sibling, group(both, 1 - core, d)

    def start(half, kind, p):
        ref, device, _ = moved(half, kind, p)
        copy(ref, many, (12 * half + kind, p), device).start()

    def arrived(half, kind, p):
        copy(moved(half, kind, p)[2], many, (12 * half + kind, p), sibling).wait_recv()

    def sent(half, kind, p):
        ref, device, _ = moved(half, kind, p)
        copy(ref, many, (12 * half + kind, p), device).wait_send()

    def left_moved(kind, q):
        before, after, far = (c + 3) % 4, (c + 1) % 4, (c + 2) % 4
        if kind == 0:
            return code.at[q, c], along_x(1), code.at[q, before]
        if kind == 1:
            return code.at[q, c], along_x(3), code.at[q, after]
        if kind == 2:
            return code.at[q, before, 0], along_x(1), code.at[q, far, 0]
        return code.at[q, after, 1], along_x(3), code.at[q, far, 1]

    def left_start(kind, q):
        ref, device, _ = left_moved(kind, q)
        copy(ref, lefts, (kind, q), device).start()

    def left_arrived(kind, q):
        copy(left_moved(kind, q)[2], lefts, (kind, q), sibling).wait_recv()

    def left_sent(kind, q):
        ref, device, _ = left_moved(kind, q)
        copy(ref, lefts, (kind, q), device).wait_send()

    def own_start(p):
        for half in (0, 1):
            start(half, 0, p)
            start(half, 1, p)

    def own_forward(p):
        for half in (0, 1):
            arrived(half, 0, p)
            start(half, 2, p)
            arrived(half, 1, p)
            start(half, 3, p)

    pl.semaphore_wait(barrier, 7)
    own_start(0)
    own_start(1)
    for one in staged:
        one.wait()

    weights = [
        [jnp.where(ids[s] == v, 1.0, 0.0).astype(jnp.float32) for s in range(slices)]
        for v in range(values)
    ]

    def encode(q, carry):
        here = pl.ds(pl.multiple_of(q * rows, rows), rows)
        blocks = [left[s, here, :].astype(jnp.float32) for s in range(slices)]
        for v in range(values):
            total = blocks[0] * weights[v][0]
            for s in range(1, slices):
                total = total + blocks[s] * weights[v][s]
            top = jnp.max(jnp.abs(total), axis=0, keepdims=True)
            top = jnp.maximum(top, 2.0**-110)
            level = jnp.ceil(jnp.log(top) * (STEPS_PER_OCTAVE / LN2))
            scale = jnp.exp(level * (-LN2 / STEPS_PER_OCTAVE)) * CODE_TOP
            code[q, c, v, :rows, :] = jnp.round(total * scale).astype(jnp.int32).astype(jnp.int16)
            code[q, c, v, rows:, :] = jnp.broadcast_to(level, (16, part_k)).astype(jnp.int32).astype(jnp.int16)

        @pl.when(q < 2)
        def _():
            left_start(0, q)
            left_start(1, q)

        return carry

    lax.fori_loop(0, 2, encode, 0)
    own_forward(0)
    lax.fori_loop(2, ROW_CHUNKS, encode, 0)

    place_at = lax.broadcasted_iota(jnp.int32, (8, bond), 1)
    j = place_at & 15
    at_y, at_z, plane = (place_at >> 4) & 3, (place_at >> 6) & 3, place_at >> 8
    shard = at_z * 8 + (at_y >> 1) * 4 + plane * 2 + (at_y & 1)
    logical = shard * shard_k + j
    stored = jnp.zeros((8, bond), jnp.int32)
    for bit in range(order.shape[0]):
        stored = stored + ((logical >> bit) & 1) * jnp.left_shift(jnp.int32(1), order[bit])
    hit = lax.broadcasted_iota(jnp.int32, (bond, bond), 0) == stored[:1]
    pick[...] = jnp.where(hit, 1.0, 0.0).astype(jnp.bfloat16)

    def decode(q):
        parts = []
        for v in range(values):
            high, low = [], []
            for at in range(4):
                level = code[q, at, v, rows:, :].astype(jnp.int32).astype(jnp.float32)[:1]
                scale = jnp.exp(level * (LN2 / STEPS_PER_OCTAVE)) * (1.0 / CODE_TOP)
                x = code[q, at, v, :rows, :].astype(jnp.int32).astype(jnp.float32) * scale
                h = x.astype(jnp.bfloat16)
                high.append(h)
                low.append((x - h.astype(jnp.float32)).astype(jnp.bfloat16))
            parts += [jnp.concatenate(high, axis=1), jnp.concatenate(low, axis=1)]
        picked = jnp.dot(
            jnp.concatenate(parts, axis=0), pick[...], preferred_element_type=jnp.float32
        ).astype(jnp.bfloat16)
        for v in range(values):
            a_ref[q, :, v * bond : (v + 1) * bond] = picked[2 * rows * v : 2 * rows * (v + 1)]

    def tile(q, p):
        here = pl.ds(pl.multiple_of(q * rows, rows), rows)
        cols = pl.ds(pl.multiple_of(p * width, width), width)
        part_ref[here, cols] = tile_product(a_ref, b_ref, q, p, width)

    def turn(u, carry):
        @pl.when(u < PAIRS - 1)
        def _():
            own_forward(u + 1)

        @pl.when(u < PAIRS - 2)
        def _():
            own_start(u + 2)

        @pl.when(u < PAIRS)
        def _():
            for half in (0, 1):
                arrived(half, 2, u)
                arrived(half, 3, u)
                start(half, 4, u)
                start(half, 5, u)
                start(half, 8, u)

        @pl.when(u < ROW_CHUNKS)
        def _():
            left_arrived(0, u)
            left_start(2, u)
            left_arrived(1, u)
            left_start(3, u)

        @pl.when(u < ROW_CHUNKS - 2)
        def _():
            left_start(0, u + 2)
            left_start(1, u + 2)

        @pl.when((u >= 1) & (u < PAIRS + 1))
        def _():
            for half in (0, 1):
                arrived(half, 4, u - 1)
                start(half, 6, u - 1)
                start(half, 9, u - 1)
                arrived(half, 5, u - 1)
                start(half, 7, u - 1)
                start(half, 10, u - 1)

        @pl.when((u >= 1) & (u < ROW_CHUNKS + 1))
        def _():
            left_arrived(2, u - 1)
            left_arrived(3, u - 1)
            decode(u - 1)

        @pl.when((u >= 2) & (u < PAIRS + 2))
        def _():
            for half in (0, 1):
                arrived(half, 6, u - 2)
                arrived(half, 7, u - 2)
                start(half, 11, u - 2)

        @pl.when(u >= 3)
        def _():
            for half in (0, 1):
                for kind in (8, 9, 10, 11):
                    arrived(half, kind, u - 3)

        @pl.when((u >= 3) & (u < EARLY + 3))
        def _():
            def one(k, carry):
                late = (u == 4) & (k == 0)
                tile(jnp.where(late, ROW_CHUNKS - 1, k - (u == 4).astype(jnp.int32)), jnp.where(late, 0, u - 3))
                return carry

            lax.fori_loop(0, jnp.where(u == 3, ROW_CHUNKS - 1, jnp.where(u == 4, ROW_CHUNKS + 1, ROW_CHUNKS)), one, 0)

        return carry

    lax.fori_loop(0, PAIRS + 3, turn, 0)

    def settle(p, carry):
        for half in (0, 1):
            for kind in range(12):
                sent(half, kind, p)
        return carry

    lax.fori_loop(0, PAIRS, settle, 0)

    def left_settle(q, carry):
        for kind in range(4):
            left_sent(kind, q)
        return carry

    lax.fori_loop(0, ROW_CHUNKS, left_settle, 0)


def finish_kernel(a_ref, b_ref, part_ref, out_ref, last, sems):
    tiles, rows, width = last.shape
    done = pltpu.make_async_copy(part_ref, out_ref.at[:, : part_ref.shape[1]], sems.at[tiles])
    done.start()

    def out_copy(n):
        here = pl.ds(pl.multiple_of(n % ROW_CHUNKS * rows, rows), rows)
        cols = pl.ds(pl.multiple_of((n // ROW_CHUNKS + EARLY) * width, width), width)
        return pltpu.make_async_copy(last.at[n], out_ref.at[here, cols], sems.at[n])

    def one(n, carry):
        last[n] = tile_product(a_ref, b_ref, n % ROW_CHUNKS, n // ROW_CHUNKS + EARLY, width)
        out_copy(n).start()
        return carry

    def settle(n, carry):
        out_copy(n).wait()
        return carry

    lax.fori_loop(0, tiles, one, 0)
    lax.fori_loop(0, tiles, settle, 0)
    done.wait()


def per_device(left_block, right_block, slice_ids, mode_order):
    slices, rows_all, part_k = left_block.shape
    shard_k, values, columns = right_block.shape
    rows, width = rows_all // ROW_CHUNKS, columns // PAIRS
    bond = 4 * part_k
    late = (PAIRS - EARLY) * ROW_CHUNKS
    right = jnp.transpose(right_block, (1, 0, 2))
    vmem = pl.BlockSpec(memory_space=pltpu.VMEM)
    hbm = pl.BlockSpec(memory_space=pltpu.HBM)
    a, b, part = pl.pallas_call(
        gather_kernel,
        out_shape=(
            pltpu.VMEM((ROW_CHUNKS, 2 * rows, values * bond), jnp.bfloat16),
            pltpu.VMEM((values, 2, 4, 4, shard_k, columns), jnp.bfloat16),
            pltpu.VMEM((rows_all, EARLY * width), jnp.float32),
        ),
        in_specs=[hbm, hbm, hbm, vmem],
        out_specs=(vmem, vmem, vmem),
        scratch_shapes=[
            pltpu.SMEM(slice_ids.shape, jnp.int32),
            pltpu.SMEM(mode_order.shape, jnp.int32),
            pltpu.VMEM(left_block.shape, left_block.dtype),
            pltpu.VMEM((ROW_CHUNKS, 4, values, rows + 16, part_k), jnp.int16),
            pltpu.VMEM((bond, bond), jnp.bfloat16),
            pltpu.SemaphoreType.DMA((3,)),
            pltpu.SemaphoreType.DMA((24, PAIRS)),
            pltpu.SemaphoreType.DMA((24, PAIRS)),
            pltpu.SemaphoreType.DMA((4, ROW_CHUNKS)),
            pltpu.SemaphoreType.DMA((4, ROW_CHUNKS)),
        ],
        compiler_params=pltpu.CompilerParams(
            collective_id=0, has_side_effects=True, vmem_limit_bytes=20 << 20
        ),
    )(*(pltpu.with_memory_space_constraint(x, pltpu.HBM) for x in (slice_ids, mode_order, left_block)), right)
    return pl.pallas_call(
        finish_kernel,
        out_shape=jax.ShapeDtypeStruct((rows_all, columns), jnp.float32),
        in_specs=[vmem, vmem, vmem],
        out_specs=pl.BlockSpec(memory_space=pl.ANY),
        scratch_shapes=[
            pltpu.VMEM((late, rows, width), jnp.float32),
            pltpu.SemaphoreType.DMA((late + 1,)),
        ],
        compiler_params=pltpu.CompilerParams(vmem_limit_bytes=20 << 20),
    )(a, b, part)


def solution(mesh):
    in_specs = (P(None, ("row", "depth"), "col"), P(("row", "depth"), None, "col"), P(), P())
    out_specs = P(("row", "depth"), "col")
    return jax.shard_map(
        per_device, mesh=mesh, in_specs=in_specs, out_specs=out_specs, check_vma=False
    )
```

time: 201 us -> 54.6 us (0.27)
  the two profiles are of different devices: /device:TPU:1 before, /device:TPU:0 now
where the time goes in v2:
time: 54.6 us; the launch traced here: 54.4 us
  Pallas kernels  53.3 us (98%)
  local copies, waits for them, and re-layouts  1.1 us (2%)
    pallas_call x1, Pallas kernels, per_device(): pl.pallas_call(gather_kernel, out_shape=(pltpu.VMEM((ROW_CHUNKS, 2 * rows...  47.2 us
    pallas_call x1, Pallas kernels, per_device(): pl.pallas_call(finish_kernel, out_shape=jax.ShapeDtypeStruct((rows_all, c...  6.1 us
    unnamed x1, local copies, waits for them, and re-layouts  1.1 us

profile of v2, /device:TPU:0, one launch (start us, length us, event | category | flops | bytes accessed | tf_op | source)
XLA Modules:
  0.0 54.4 jit_solution(7421574167268004330)
XLA Ops:
  0.0 1.1 %copy.7 = bf16[16,2,4096]{2,0,1:T(8,128)(2,1)S(1)} copy(bf16[16,2,4096]{2,1,0:T(2,128)(2,1)} %param.5) | data formatting | bytes 524288 | tf_op args[1]
  1.1 47.2 %shard_map.46 = (bf16[4,512,1024]{2,1,0:T(8,128)(2,1)S(1)}, bf16[2,2,4,4,16,4096]{5,4,3,2,1,0:T(8,128)(2,1)S(1)}, f32[1024,3072]{1,0:T(8,128)S(1)}) custom-call(s32[4]{0:T(128)} %ids_hbm.1, s32[9]{0:T(128)} %order_hbm.1, bf16[4,1024,128]{2,1,0:T(8,128)(2,1)} %left_hbm.1, bf16[2,16,4096]{2,1,0:T(8,128)(2,1)S(1)} %bitcast.3), custom_call_target="tpu_custom_call" | custom-call | tf_op jit(solution)/shard_map/pallas_call | solution.py:368
  48.3 6.1 %shard_map.47 = f32[1024,4096]{1,0:T(8,128)} custom-call(bf16[4,512,1024]{2,1,0:T(8,128)(2,1)S(1)} %get-tuple-element.8.a_ref, bf16[2,2,4,4,16,4096]{5,4,3,2,1,0:T(8,128)(2,1)S(1)} %get-tuple-element.9.b_ref, f32[1024,3072]{1,0:T(8,128)S(1)} %get-tuple-element.10.part_ref), custom_call_target="tpu_custom_call" | custom-call | tf_op jit(solution)/shard_map/pallas_call | solution.py:393

commit v3 on v2

--- a/solution.py
+++ b/solution.py
@@ -175,8 +175,8 @@
             start(half, 3, p)
 
     pl.semaphore_wait(barrier, 7)
-    own_start(0)
-    own_start(1)
+    for p in range(PAIRS):
+        own_start(p)
     for one in staged:
         one.wait()
 
@@ -207,7 +207,8 @@
         return carry
 
     lax.fori_loop(0, 2, encode, 0)
-    own_forward(0)
+    for p in range(PAIRS):
+        own_forward(p)
     lax.fori_loop(2, ROW_CHUNKS, encode, 0)
 
     place_at = lax.broadcasted_iota(jnp.int32, (8, bond), 1)
@@ -244,77 +245,87 @@
         cols = pl.ds(pl.multiple_of(p * width, width), width)
         part_ref[here, cols] = tile_product(a_ref, b_ref, q, p, width)
 
-    def turn(u, carry):
-        @pl.when(u < PAIRS - 1)
-        def _():
-            own_forward(u + 1)
-
-        @pl.when(u < PAIRS - 2)
-        def _():
-            own_start(u + 2)
-
-        @pl.when(u < PAIRS)
-        def _():
-            for half in (0, 1):
-                arrived(half, 2, u)
-                arrived(half, 3, u)
-                start(half, 4, u)
-                start(half, 5, u)
-                start(half, 8, u)
-
-        @pl.when(u < ROW_CHUNKS)
-        def _():
-            left_arrived(0, u)
-            left_start(2, u)
-            left_arrived(1, u)
-            left_start(3, u)
-
-        @pl.when(u < ROW_CHUNKS - 2)
-        def _():
-            left_start(0, u + 2)
-            left_start(1, u + 2)
-
-        @pl.when((u >= 1) & (u < PAIRS + 1))
-        def _():
-            for half in (0, 1):
-                arrived(half, 4, u - 1)
-                start(half, 6, u - 1)
-                start(half, 9, u - 1)
-                arrived(half, 5, u - 1)
-                start(half, 7, u - 1)
-                start(half, 10, u - 1)
-
-        @pl.when((u >= 1) & (u < ROW_CHUNKS + 1))
-        def _():
-            left_arrived(2, u - 1)
-            left_arrived(3, u - 1)
-            decode(u - 1)
-
-        @pl.when((u >= 2) & (u < PAIRS + 2))
-        def _():
-            for half in (0, 1):
-                arrived(half, 6, u - 2)
-                arrived(half, 7, u - 2)
-                start(half, 11, u - 2)
-
-        @pl.when(u >= 3)
-        def _():
-            for half in (0, 1):
-                for kind in (8, 9, 10, 11):
-                    arrived(half, kind, u - 3)
-
-        @pl.when((u >= 3) & (u < EARLY + 3))
-        def _():
-            def one(k, carry):
-                late = (u == 4) & (k == 0)
-                tile(jnp.where(late, ROW_CHUNKS - 1, k - (u == 4).astype(jnp.int32)), jnp.where(late, 0, u - 3))
-                return carry
-
-            lax.fori_loop(0, jnp.where(u == 3, ROW_CHUNKS - 1, jnp.where(u == 4, ROW_CHUNKS + 1, ROW_CHUNKS)), one, 0)
-
-        return carry
-
-    lax.fori_loop(0, PAIRS + 3, turn, 0)
+    def tiles(q_from, q_to, p_from, p_to):
+        many_q = q_to - q_from
+
+        def one(n, carry):
+            tile(q_from + n % many_q, p_from + n // many_q)
+            return carry
+
+        lax.fori_loop(0, many_q * (p_to - p_from), one, 0)
+
+    def group_start(p):
+        for half in (0, 1):
+            arrived(half, 2, p)
+            arrived(half, 3, p)
+            start(half, 4, p)
+            start(half, 5, p)
+            start(half, 8, p)
+
+    def group_forward(p):
+        for half in (0, 1):
+            arrived(half, 4, p)
+            start(half, 6, p)
+            start(half, 9, p)
+            arrived(half, 5, p)
+            start(half, 7, p)
+            start(half, 10, p)
+
+    def group_last(p):
+        for half in (0, 1):
+            arrived(half, 6, p)
+            arrived(half, 7, p)
+            start(half, 11, p)
+
+    def whole(p):
+        for half in (0, 1):
+            for kind in (8, 9, 10, 11):
+                arrived(half, kind, p)
+
+    def left_forward(q):
+        left_arrived(0, q)
+        left_start(2, q)
+        left_arrived(1, q)
+        left_start(3, q)
+        if q + 2 < ROW_CHUNKS:
+            left_start(0, q + 2)
+            left_start(1, q + 2)
+
+    def left_whole(q):
+        left_arrived(2, q)
+        left_arrived(3, q)
+        decode(q)
+
+    group_start(0)
+    group_start(1)
+    left_forward(0)
+    group_forward(0)
+    group_start(2)
+    left_forward(1)
+    left_whole(0)
+    group_forward(1)
+    group_start(3)
+    left_forward(2)
+    group_last(0)
+    whole(0)
+    tiles(0, 1, 0, 1)
+    left_whole(1)
+    left_forward(3)
+    tiles(1, 2, 0, 1)
+    group_forward(2)
+    group_last(1)
+    whole(1)
+    tiles(0, 2, 1, 2)
+    group_forward(3)
+    group_last(2)
+    left_whole(2)
+    tiles(2, 3, 0, 2)
+    whole(2)
+    group_last(3)
+    tiles(0, 3, 2, 3)
+    left_whole(3)
+    tiles(3, 4, 0, 3)
+    whole(3)
 
     def settle(p, carry):
         for half in (0, 1):

time: 54.6 us -> 55.1 us (level)
  the two profiles are of different devices: /device:TPU:0 before, /device:TPU:1 now
where the time goes in v3:
time: 55.1 us; the launch traced here: 54.5 us
  Pallas kernels  53.4 us (97%)
  local copies, waits for them, and re-layouts  1.1 us (2%)
    pallas_call x1, Pallas kernels, per_device(): pl.pallas_call(gather_kernel, out_shape=(pltpu.VMEM((ROW_CHUNKS, 2 * rows...  47.3 us
    pallas_call x1, Pallas kernels, per_device(): pl.pallas_call(finish_kernel, out_shape=jax.ShapeDtypeStruct((rows_all, c...  6.1 us

profile of v3, /device:TPU:1, one launch (start us, length us, event | category | flops | bytes accessed | tf_op | source)
XLA Modules:
  0.0 54.5 jit_solution(16874945233370372065)
XLA Ops:
  0.0 1.1 %copy.7 = bf16[16,2,4096]{2,0,1:T(8,128)(2,1)S(1)} copy(bf16[16,2,4096]{2,1,0:T(2,128)(2,1)} %param.5) | data formatting | bytes 524288 | tf_op args[1]
  1.1 47.3 %shard_map.46 = (bf16[4,512,1024]{2,1,0:T(8,128)(2,1)S(1)}, bf16[2,2,4,4,16,4096]{5,4,3,2,1,0:T(8,128)(2,1)S(1)}, f32[1024,3072]{1,0:T(8,128)S(1)}) custom-call(s32[4]{0:T(128)} %ids_hbm.1, s32[9]{0:T(128)} %order_hbm.1, bf16[4,1024,128]{2,1,0:T(8,128)(2,1)} %left_hbm.1, bf16[2,16,4096]{2,1,0:T(8,128)(2,1)S(1)} %bitcast.3), custom_call_target="tpu_custom_call" | custom-call | tf_op jit(solution)/shard_map/pallas_call | solution.py:379
  48.4 6.1 %shard_map.47 = f32[1024,4096]{1,0:T(8,128)} custom-call(bf16[4,512,1024]{2,1,0:T(8,128)(2,1)S(1)} %get-tuple-element.8.a_ref, bf16[2,2,4,4,16,4096]{5,4,3,2,1,0:T(8,128)(2,1)S(1)} %get-tuple-element.9.b_ref, f32[1024,3072]{1,0:T(8,128)S(1)} %get-tuple-element.10.part_ref), custom_call_target="tpu_custom_call" | custom-call | tf_op jit(solution)/shard_map/pallas_call | solution.py:404

commit v4 on v3

--- a/solution.py
+++ b/solution.py
@@ -11,17 +11,18 @@
 MESH = pl.DeviceIdType.MESH
 ROW_CHUNKS = 4
 PAIRS = 4
+AHEAD = 2
 EARLY = 3
 CODE_TOP = 32000.0
 STEPS_PER_OCTAVE = 16.0
 LN2 = math.log(2.0)
 
 
-def tile_product(a_ref, b_ref, i, j, width):
-    cols = pl.ds(pl.multiple_of(j * width, width), width)
-    b = b_ref[:, :, :, :, :, cols]
-    b = b.reshape(-1, width)
-    both = jnp.dot(a_ref[i], b, preferred_element_type=jnp.float32)
+def tile_product(a_ref, b_ref, q, p):
+    halves = [b_ref[p, half] for half in (0, 1)]
+    strip = halves[0].shape[-1]
+    b = jnp.concatenate([half.reshape(-1, strip) for half in halves], axis=1)
+    both = jnp.dot(a_ref[q], b, preferred_element_type=jnp.float32)
     rows = both.shape[0] // 2
     return both[:rows] + both[rows:]
 
@@ -42,7 +43,6 @@
     local,
     send,
     recv,
-    left_send,
     left_recv,
 ):
     slices, rows_all, part_k = left.shape
@@ -81,36 +81,36 @@
     ]
     for one in staged:
         one.start()
-    b_ref[:, core, z, y] = right_ref[...]
-
-    def copy(ref, sems, at, device):
+    for p in range(PAIRS):
+        for half in (0, 1):
+            at = p * width + half * strip
+            b_ref[p, half, :, core, z, y] = right_ref[:, :, at : at + strip]
+
+    def copy(ref, signals, device):
         return pltpu.make_async_remote_copy(
             src_ref=ref,
             dst_ref=ref,
-            send_sem=sems[0].at[at],
-            recv_sem=sems[1].at[at],
+            send_sem=signals[0],
+            recv_sem=signals[1],
             device_id=device,
             device_id_type=MESH,
         )
 
-    many, lefts = (send, recv), (left_send, left_recv)
-
     def moved(half, kind, p):
-        cols = pl.ds(pl.multiple_of(p * width + half * strip, strip), strip)
         first, second = (along_y, along_z) if half == 0 else (along_z, along_y)
         at1, at2 = (y, z) if half == 0 else (z, y)
+        both = slice(None)
 
         def one(v, d):
             at = (at1 + d) % 4
             where = (z, at) if half == 0 else (at, y)
-            return b_ref.at[(v, core, *where, slice(None), cols)]
-
-        def group(v, plane, d):
+            return b_ref.at[(pl.ds(p * AHEAD, AHEAD), half, v, core, *where)]
+
+        def group(v, d):
             at = (at2 + d) % 4
-            where = (at, slice(None)) if half == 0 else (slice(None), at)
-            return b_ref.at[(v, plane, *where, slice(None), cols)]
-
-        both = slice(None)
+            where = (at, both) if half == 0 else (both, at)
+            return b_ref.at[(p, half, v, core, *where)]
+
         if kind == 0:
             return one(both, 0), first(1), one(both, 3)
         if kind == 1:
@@ -120,26 +120,24 @@
         if kind == 3:
             return one(1, 1), first(3), one(1, 2)
         if kind == 4:
-            return group(both, core, 0), second(1), group(both, core, 3)
+            return group(both, 0), second(1), group(both, 3)
         if kind == 5:
-            return group(both, core, 0), second(3), group(both, core, 1)
+            return group(both, 0), second(3), group(both, 1)
         if kind == 6:
-            return group(0, core, 3), second(1), group(0, core, 2)
+            return group(0, 3), second(1), group(0, 2)
         if kind == 7:
-            return group(1, core, 1), second(3), group(1, core, 2)
-        d = (0, 3, 1, 2)[kind - 8]
-        return group(both, core, d), sibling, group(both, 1 - core, d)
+            return group(1, 1), second(3), group(1, 2)
+        return b_ref.at[p, :, :, core], sibling, b_ref.at[p, :, :, 1 - core]
+
+    def sems(half, kind, p):
+        return send.at[kind // 2], recv.at[half, kind, p]
 
     def start(half, kind, p):
         ref, device, _ = moved(half, kind, p)
-        copy(ref, many, (12 * half + kind, p), device).start()
+        copy(ref, sems(half, kind, p), device).start()
 
     def arrived(half, kind, p):
-        copy(moved(half, kind, p)[2], many, (12 * half + kind, p), sibling).wait_recv()
-
-    def sent(half, kind, p):
-        ref, device, _ = moved(half, kind, p)
-        copy(ref, many, (12 * half + kind, p), device).wait_send()
+        copy(moved(half, kind, p)[2], sems(half, kind, p), sibling).wait_recv()
 
     def left_moved(kind, q):
         before, after, far = (c + 3) % 4, (c + 1) % 4, (c + 2) % 4
@@ -151,16 +149,15 @@
             return code.at[q, before, 0], along_x(1), code.at[q, far, 0]
         return code.at[q, after, 1], along_x(3), code.at[q, far, 1]
 
+    def left_sems(kind, q):
+        return send.at[5 + kind // 2], left_recv.at[kind, q]
+
     def left_start(kind, q):
         ref, device, _ = left_moved(kind, q)
-        copy(ref, lefts, (kind, q), device).start()
+        copy(ref, left_sems(kind, q), device).start()
 
     def left_arrived(kind, q):
-        copy(left_moved(kind, q)[2], lefts, (kind, q), sibling).wait_recv()
-
-    def left_sent(kind, q):
-        ref, device, _ = left_moved(kind, q)
-        copy(ref, lefts, (kind, q), device).wait_send()
+        copy(left_moved(kind, q)[2], left_sems(kind, q), sibling).wait_recv()
 
     def own_start(p):
         for half in (0, 1):
@@ -175,7 +172,7 @@
             start(half, 3, p)
 
     pl.semaphore_wait(barrier, 7)
-    for p in range(PAIRS):
+    for p in range(PAIRS // AHEAD):
         own_start(p)
     for one in staged:
         one.wait()
@@ -207,7 +204,7 @@
         return carry
 
     lax.fori_loop(0, 2, encode, 0)
-    for p in range(PAIRS):
+    for p in range(PAIRS // AHEAD):
         own_forward(p)
     lax.fori_loop(2, ROW_CHUNKS, encode, 0)
 
@@ -243,7 +240,7 @@
     def tile(q, p):
         here = pl.ds(pl.multiple_of(q * rows, rows), rows)
         cols = pl.ds(pl.multiple_of(p * width, width), width)
-        part_ref[here, cols] = tile_product(a_ref, b_ref, q, p, width)
+        part_ref[here, cols] = tile_product(a_ref, b_ref, q, p)
 
     def tiles(q_from, q_to, p_from, p_to):
         many_q = q_to - q_from
@@ -256,31 +253,27 @@
 
     def group_start(p):
         for half in (0, 1):
-            arrived(half, 2, p)
-            arrived(half, 3, p)
+            if p % AHEAD == 0:
+                arrived(half, 2, p // AHEAD)
+                arrived(half, 3, p // AHEAD)
             start(half, 4, p)
             start(half, 5, p)
-            start(half, 8, p)
 
     def group_forward(p):
         for half in (0, 1):
             arrived(half, 4, p)
             start(half, 6, p)
-            start(half, 9, p)
             arrived(half, 5, p)
             start(half, 7, p)
-            start(half, 10, p)
 
     def group_last(p):
         for half in (0, 1):
             arrived(half, 6, p)
             arrived(half, 7, p)
-            start(half, 11, p)
+        start(0, 8, p)
 
     def whole(p):
-        for half in (0, 1):
-            for kind in (8, 9, 10, 11):
-                arrived(half, kind, p)
+        arrived(0, 8, p)
 
     def left_forward(q):
         left_arrived(0, q)
@@ -327,20 +320,17 @@
     tiles(3, 4, 0, 3)
     whole(3)
 
-    def settle(p, carry):
-        for half in (0, 1):
-            for kind in range(12):
-                sent(half, kind, p)
-        return carry
-
-    lax.fori_loop(0, PAIRS, settle, 0)
-
-    def left_settle(q, carry):
-        for kind in range(4):
-            left_sent(kind, q)
-        return carry
-
-    lax.fori_loop(0, ROW_CHUNKS, left_settle, 0)
+    sizes = (
+        b_ref.at[0, 0, 0],
+        b_ref.at[0, 0, 0, 0],
+        b_ref.at[0],
+        b_ref.at[0, 0],
+        b_ref.at[pl.ds(0, PAIRS // 2)],
+        code.at[pl.ds(0, 2)],
+        code.at[0],
+    )
+    for n, size in enumerate(sizes):
+        copy(size, (send.at[n], recv.at[0, 0, 0]), sibling).wait_send()
 
 
 def finish_kernel(a_ref, b_ref, part_ref, out_ref, last, sems):
@@ -354,7 +344,7 @@
         return pltpu.make_async_copy(last.at[n], out_ref.at[here, cols], sems.at[n])
 
     def one(n, carry):
-        last[n] = tile_product(a_ref, b_ref, n % ROW_CHUNKS, n // ROW_CHUNKS + EARLY, width)
+        last[n] = tile_product(a_ref, b_ref, n % ROW_CHUNKS, n // ROW_CHUNKS + EARLY)
         out_copy(n).start()
         return carry
 
@@ -380,7 +370,7 @@
         gather_kernel,
         out_shape=(
             pltpu.VMEM((ROW_CHUNKS, 2 * rows, values * bond), jnp.bfloat16),
-            pltpu.VMEM((values, 2, 4, 4, shard_k, columns), jnp.bfloat16),
+            pltpu.VMEM((PAIRS, 2, values, 2, 4, 4, shard_k, width // 2), jnp.bfloat16),
             pltpu.VMEM((rows_all, EARLY * width), jnp.float32),
         ),
         in_specs=[hbm, hbm, hbm, vmem],
@@ -392,9 +382,8 @@
             pltpu.VMEM((ROW_CHUNKS, 4, values, rows + 16, part_k), jnp.int16),
             pltpu.VMEM((bond, bond), jnp.bfloat16),
             pltpu.SemaphoreType.DMA((3,)),
-            pltpu.SemaphoreType.DMA((24, PAIRS)),
-            pltpu.SemaphoreType.DMA((24, PAIRS)),
-            pltpu.SemaphoreType.DMA((4, ROW_CHUNKS)),
+            pltpu.SemaphoreType.DMA((7,)),
+            pltpu.SemaphoreType.DMA((2, 9, PAIRS)),
             pltpu.SemaphoreType.DMA((4, ROW_CHUNKS)),
         ],
         compiler_params=pltpu.CompilerParams(

time: 55.1 us -> 55.8 us (1.013)
  Pallas kernels: 53.4 us -> 54.4 us
    pallas_call x1, Pallas kernels: 47.3 us -> 48.3 us  [per_device(): pl.pallas_call(gather_kernel, out_shape=(pltpu.VMEM((ROW_CHUNKS, 2 * rows...]
where the time goes in v4:
time: 55.8 us; the launch traced here: 55.5 us
  Pallas kernels  54.4 us (97%)
  local copies, waits for them, and re-layouts  1.1 us (2%)
    pallas_call x1, Pallas kernels, per_device(): pl.pallas_call(gather_kernel, out_shape=(pltpu.VMEM((ROW_CHUNKS, 2 * rows...  48.3 us
    pallas_call x1, Pallas kernels, per_device(): pl.pallas_call(finish_kernel, out_shape=jax.ShapeDtypeStruct((rows_all, c...  6.1 us

profile of v4, /device:TPU:1, one launch (start us, length us, event | category | flops | bytes accessed | tf_op | source)
XLA Modules:
  0.0 55.5 jit_solution(3893294344380960064)
XLA Ops:
  0.0 1.1 %copy.7 = bf16[16,2,4096]{2,0,1:T(8,128)(2,1)S(1)} copy(bf16[16,2,4096]{2,1,0:T(2,128)(2,1)} %param.5) | data formatting | bytes 524288 | tf_op args[1]
  1.1 48.3 %shard_map.46 = (bf16[4,512,1024]{2,1,0:T(8,128)(2,1)S(1)}, bf16[4,2,2,2,4,4,16,512]{7,6,5,4,3,2,1,0:T(8,128)(2,1)S(1)}, f32[1024,3072]{1,0:T(8,128)S(1)}) custom-call(s32[4]{0:T(128)} %ids_hbm.1, s32[9]{0:T(128)} %order_hbm.1, bf16[4,1024,128]{2,1,0:T(8,128)(2,1)} %left_hbm.1, bf16[2,16,4096]{2,1,0:T(8,128)(2,1)S(1)} %bitcast.3), custom_call_target="tpu_custom_call" | custom-call | tf_op jit(solution)/shard_map/pallas_call | solution.py:369
  49.4 6.1 %shard_map.47 = f32[1024,4096]{1,0:T(8,128)} custom-call(bf16[4,512,1024]{2,1,0:T(8,128)(2,1)S(1)} %get-tuple-element.8.a_ref, bf16[4,2,2,2,4,4,16,512]{7,6,5,4,3,2,1,0:T(8,128)(2,1)S(1)} %get-tuple-element.9.b_ref, f32[1024,3072]{1,0:T(8,128)S(1)} %get-tuple-element.10.part_ref), custom_call_target="tpu_custom_call" | custom-call | tf_op jit(solution)/shard_map/pallas_call | solution.py:393

commit v5 on v4

--- a/solution.py
+++ b/solution.py
@@ -10,9 +10,9 @@
 
 MESH = pl.DeviceIdType.MESH
 ROW_CHUNKS = 4
-PAIRS = 4
-AHEAD = 2
-EARLY = 3
+PAIRS = 8
+AHEAD = 4
+EARLY = 6
 CODE_TOP = 32000.0
 STEPS_PER_OCTAVE = 16.0
 LN2 = math.log(2.0)
@@ -22,9 +22,11 @@
     halves = [b_ref[p, half] for half in (0, 1)]
     strip = halves[0].shape[-1]
     b = jnp.concatenate([half.reshape(-1, strip) for half in halves], axis=1)
-    both = jnp.dot(a_ref[q], b, preferred_element_type=jnp.float32)
-    rows = both.shape[0] // 2
-    return both[:rows] + both[rows:]
+    a = a_ref[pl.ds(2 * q, 2)]
+    rows = a.shape[1] // 2
+    both = jnp.dot(a.reshape(-1, a.shape[2]), b, preferred_element_type=jnp.float32)
+    both = both.reshape(2, 2, rows, both.shape[1])
+    return (both[:, 0] + both[:, 1]).reshape(2 * rows, both.shape[3])
 
 
 def gather_kernel(
@@ -238,18 +240,7 @@
             a_ref[q, :, v * bond : (v + 1) * bond] = picked[2 * rows * v : 2 * rows * (v + 1)]
 
     def tile(q, p):
-        here = pl.ds(pl.multiple_of(q * rows, rows), rows)
-        cols = pl.ds(pl.multiple_of(p * width, width), width)
-        part_ref[here, cols] = tile_product(a_ref, b_ref, q, p)
-
-    def tiles(q_from, q_to, p_from, p_to):
-        many_q = q_to - q_from
-
-        def one(n, carry):
-            tile(q_from + n % many_q, p_from + n // many_q)
-            return carry
-
-        lax.fori_loop(0, many_q * (p_to - p_from), one, 0)
+        part_ref[2 * q * rows : 2 * (q + 1) * rows, p * width : (p + 1) * width] = tile_product(a_ref, b_ref, q, p)
 
     def group_start(p):
         for half in (0, 1):
@@ -296,35 +287,34 @@
     group_start(2)
     left_forward(1)
     left_whole(0)
-    group_forward(1)
-    group_start(3)
-    left_forward(2)
-    group_last(0)
-    whole(0)
-    tiles(0, 1, 0, 1)
-    left_whole(1)
-    left_forward(3)
-    tiles(1, 2, 0, 1)
-    group_forward(2)
-    group_last(1)
-    whole(1)
-    tiles(0, 2, 1, 2)
-    group_forward(3)
-    group_last(2)
-    left_whole(2)
-    tiles(2, 3, 0, 2)
-    whole(2)
-    group_last(3)
-    tiles(0, 3, 2, 3)
-    left_whole(3)
-    tiles(3, 4, 0, 3)
-    whole(3)
+    for p in range(PAIRS):
+        if p + 1 < PAIRS:
+            group_forward(p + 1)
+        if p + 3 < PAIRS:
+            group_start(p + 3)
+        group_last(p)
+        if p == 0:
+            left_forward(2)
+            left_whole(1)
+        if p == 1:
+            left_forward(3)
+        if p == 2:
+            left_whole(2)
+            left_whole(3)
+            tile(1, 0)
+        if p == 3:
+            tile(1, 1)
+        if 3 <= p <= EARLY:
+            tile(1, p - 1)
+        whole(p)
+        if p < EARLY:
+            tile(0, p)
 
     sizes = (
+        b_ref.at[0, 0],
         b_ref.at[0, 0, 0],
-        b_ref.at[0, 0, 0, 0],
+        b_ref.at[pl.ds(0, PAIRS // 4)],
         b_ref.at[0],
-        b_ref.at[0, 0],
         b_ref.at[pl.ds(0, PAIRS // 2)],
         code.at[pl.ds(0, 2)],
         code.at[0],
@@ -339,12 +329,12 @@
     done.start()
 
     def out_copy(n):
-        here = pl.ds(pl.multiple_of(n % ROW_CHUNKS * rows, rows), rows)
-        cols = pl.ds(pl.multiple_of((n // ROW_CHUNKS + EARLY) * width, width), width)
+        here = pl.ds(pl.multiple_of(n % 2 * rows, rows), rows)
+        cols = pl.ds(pl.multiple_of((n // 2 + EARLY) * width, width), width)
         return pltpu.make_async_copy(last.at[n], out_ref.at[here, cols], sems.at[n])
 
     def one(n, carry):
-        last[n] = tile_product(a_ref, b_ref, n % ROW_CHUNKS, n // ROW_CHUNKS + EARLY)
+        last[n] = tile_product(a_ref, b_ref, n % 2, n // 2 + EARLY)
         out_copy(n).start()
         return carry
 
@@ -362,7 +352,7 @@
     shard_k, values, columns = right_block.shape
     rows, width = rows_all // ROW_CHUNKS, columns // PAIRS
     bond = 4 * part_k
-    late = (PAIRS - EARLY) * ROW_CHUNKS
+    late = (PAIRS - EARLY) * 2
     right = jnp.transpose(right_block, (1, 0, 2))
     vmem = pl.BlockSpec(memory_space=pltpu.VMEM)
     hbm = pl.BlockSpec(memory_space=pltpu.HBM)
@@ -396,7 +386,7 @@
         in_specs=[vmem, vmem, vmem],
         out_specs=pl.BlockSpec(memory_space=pl.ANY),
         scratch_shapes=[
-            pltpu.VMEM((late, rows, width), jnp.float32),
+            pltpu.VMEM((late, rows_all // 2, width), jnp.float32),
             pltpu.SemaphoreType.DMA((late + 1,)),
         ],
         compiler_params=pltpu.CompilerParams(vmem_limit_bytes=20 << 20),

time: 55.8 us -> 57.9 us (1.038)
  Pallas kernels: 54.4 us -> 56.7 us
    pallas_call x1, Pallas kernels: 48.3 us -> 50.6 us  [per_device(): pl.pallas_call(gather_kernel, out_shape=(pltpu.VMEM((ROW_CHUNKS, 2 * rows...]
where the time goes in v5:
time: 57.9 us; the launch traced here: 57.8 us
  Pallas kernels  56.7 us (98%)
  local copies, waits for them, and re-layouts  1.1 us (2%)
    pallas_call x1, Pallas kernels, per_device(): pl.pallas_call(gather_kernel, out_shape=(pltpu.VMEM((ROW_CHUNKS, 2 * rows...  50.6 us
    pallas_call x1, Pallas kernels, per_device(): pl.pallas_call(finish_kernel, out_shape=jax.ShapeDtypeStruct((rows_all, c...  6.1 us

profile of v5, /device:TPU:1, one launch (start us, length us, event | category | flops | bytes accessed | tf_op | source)
XLA Modules:
  0.0 57.8 jit_solution(11892582163163792556)
XLA Ops:
  0.0 1.1 %copy.7 = bf16[16,2,4096]{2,0,1:T(8,128)(2,1)S(1)} copy(bf16[16,2,4096]{2,1,0:T(2,128)(2,1)} %param.5) | data formatting | bytes 524288 | tf_op args[1]
  1.1 50.6 %shard_map.46 = (bf16[4,512,1024]{2,1,0:T(8,128)(2,1)S(1)}, bf16[8,2,2,2,4,4,16,256]{7,6,5,4,3,2,1,0:T(8,128)(2,1)S(1)}, f32[1024,3072]{1,0:T(8,128)S(1)}) custom-call(s32[4]{0:T(128)} %ids_hbm.1, s32[9]{0:T(128)} %order_hbm.1, bf16[4,1024,128]{2,1,0:T(8,128)(2,1)} %left_hbm.1, bf16[2,16,4096]{2,1,0:T(8,128)(2,1)S(1)} %bitcast.3), custom_call_target="tpu_custom_call" | custom-call | tf_op jit(solution)/shard_map/pallas_call | solution.py:359
  51.7 6.1 %shard_map.47 = f32[1024,4096]{1,0:T(8,128)} custom-call(bf16[4,512,1024]{2,1,0:T(8,128)(2,1)S(1)} %get-tuple-element.8.a_ref, bf16[8,2,2,2,4,4,16,256]{7,6,5,4,3,2,1,0:T(8,128)(2,1)S(1)} %get-tuple-element.9.b_ref, f32[1024,3072]{1,0:T(8,128)S(1)} %get-tuple-element.10.part_ref), custom_call_target="tpu_custom_call" | custom-call | tf_op jit(solution)/shard_map/pallas_call | solution.py:383

commit v6 on v4

--- a/solution.py
+++ b/solution.py
@@ -11,20 +11,22 @@
 MESH = pl.DeviceIdType.MESH
 ROW_CHUNKS = 4
 PAIRS = 4
-AHEAD = 2
+AHEAD = 1
 EARLY = 3
 CODE_TOP = 32000.0
 STEPS_PER_OCTAVE = 16.0
 LN2 = math.log(2.0)
 
 
-def tile_product(a_ref, b_ref, q, p):
-    halves = [b_ref[p, half] for half in (0, 1)]
-    strip = halves[0].shape[-1]
-    b = jnp.concatenate([half.reshape(-1, strip) for half in halves], axis=1)
-    both = jnp.dot(a_ref[q], b, preferred_element_type=jnp.float32)
-    rows = both.shape[0] // 2
-    return both[:rows] + both[rows:]
+def tile_product(a_ref, b_ref, q, p, half):
+    b = b_ref[p, half]
+    a = a_ref[pl.ds(2 * q, 2)]
+    rows = a.shape[1] // 2
+    both = jnp.dot(
+        a.reshape(-1, a.shape[2]), b.reshape(-1, b.shape[-1]), preferred_element_type=jnp.float32
+    )
+    both = both.reshape(2, 2, rows, both.shape[1])
+    return (both[:, 0] + both[:, 1]).reshape(2 * rows, both.shape[3])
 
 
 def gather_kernel(
@@ -127,7 +129,7 @@
             return group(0, 3), second(1), group(0, 2)
         if kind == 7:
             return group(1, 1), second(3), group(1, 2)
-        return b_ref.at[p, :, :, core], sibling, b_ref.at[p, :, :, 1 - core]
+        return b_ref.at[p, half, :, core], sibling, b_ref.at[p, half, :, 1 - core]
 
     def sems(half, kind, p):
         return send.at[kind // 2], recv.at[half, kind, p]
@@ -203,10 +205,7 @@
 
         return carry
 
-    lax.fori_loop(0, 2, encode, 0)
-    for p in range(PAIRS // AHEAD):
-        own_forward(p)
-    lax.fori_loop(2, ROW_CHUNKS, encode, 0)
+    lax.fori_loop(0, ROW_CHUNKS, encode, 0)
 
     place_at = lax.broadcasted_iota(jnp.int32, (8, bond), 1)
     j = place_at & 15
@@ -218,6 +217,9 @@
         stored = stored + ((logical >> bit) & 1) * jnp.left_shift(jnp.int32(1), order[bit])
     hit = lax.broadcasted_iota(jnp.int32, (bond, bond), 0) == stored[:1]
     pick[...] = jnp.where(hit, 1.0, 0.0).astype(jnp.bfloat16)
+
+    for p in range(PAIRS // AHEAD):
+        own_forward(p)
 
     def decode(q):
         parts = []
@@ -237,19 +239,9 @@
         for v in range(values):
             a_ref[q, :, v * bond : (v + 1) * bond] = picked[2 * rows * v : 2 * rows * (v + 1)]
 
-    def tile(q, p):
-        here = pl.ds(pl.multiple_of(q * rows, rows), rows)
-        cols = pl.ds(pl.multiple_of(p * width, width), width)
-        part_ref[here, cols] = tile_product(a_ref, b_ref, q, p)
-
-    def tiles(q_from, q_to, p_from, p_to):
-        many_q = q_to - q_from
-
-        def one(n, carry):
-            tile(q_from + n % many_q, p_from + n // many_q)
-            return carry
-
-        lax.fori_loop(0, many_q * (p_to - p_from), one, 0)
+    def tile(q, p, half):
+        at = p * width + half * strip
+        part_ref[2 * q * rows : 2 * (q + 1) * rows, at : at + strip] = tile_product(a_ref, b_ref, q, p, half)
 
     def group_start(p):
         for half in (0, 1):
@@ -270,10 +262,10 @@
         for half in (0, 1):
             arrived(half, 6, p)
             arrived(half, 7, p)
-        start(0, 8, p)
-
-    def whole(p):
-        arrived(0, 8, p)
+            start(half, 8, p)
+
+    def whole(p, half):
+        arrived(half, 8, p)
 
     def left_forward(q):
         left_arrived(0, q)
@@ -300,25 +292,33 @@
     group_start(3)
     left_forward(2)
     group_last(0)
-    whole(0)
-    tiles(0, 1, 0, 1)
     left_whole(1)
     left_forward(3)
-    tiles(1, 2, 0, 1)
+    whole(0, 0)
+    tile(0, 0, 0)
     group_forward(2)
+    whole(0, 1)
+    tile(0, 0, 1)
     group_last(1)
-    whole(1)
-    tiles(0, 2, 1, 2)
+    left_whole(2)
+    whole(1, 0)
+    tile(0, 1, 0)
+    whole(1, 1)
     group_forward(3)
+    tile(0, 1, 1)
+    left_whole(3)
+    tile(1, 0, 0)
+    tile(1, 0, 1)
     group_last(2)
-    left_whole(2)
-    tiles(2, 3, 0, 2)
-    whole(2)
+    tile(1, 1, 0)
     group_last(3)
-    tiles(0, 3, 2, 3)
-    left_whole(3)
-    tiles(3, 4, 0, 3)
-    whole(3)
+    tile(1, 1, 1)
+    for half in (0, 1):
+        whole(2, half)
+        tile(0, 2, half)
+        tile(1, 2, half)
+    whole(3, 0)
+    whole(3, 1)
 
     sizes = (
         b_ref.at[0, 0, 0],
@@ -339,12 +339,12 @@
     done.start()
 
     def out_copy(n):
-        here = pl.ds(pl.multiple_of(n % ROW_CHUNKS * rows, rows), rows)
-        cols = pl.ds(pl.multiple_of((n // ROW_CHUNKS + EARLY) * width, width), width)
+        here = pl.ds(pl.multiple_of(n % 2 * rows, rows), rows)
+        cols = pl.ds(pl.multiple_of((n // 2 + 2 * EARLY) * width, width), width)
         return pltpu.make_async_copy(last.at[n], out_ref.at[here, cols], sems.at[n])
 
     def one(n, carry):
-        last[n] = tile_product(a_ref, b_ref, n % ROW_CHUNKS, n // ROW_CHUNKS + EARLY)
+        last[n] = tile_product(a_ref, b_ref, n % 2, n // 4 + EARLY, n // 2 % 2)
         out_copy(n).start()
         return carry
 
@@ -362,7 +362,7 @@
     shard_k, values, columns = right_block.shape
     rows, width = rows_all // ROW_CHUNKS, columns // PAIRS
     bond = 4 * part_k
-    late = (PAIRS - EARLY) * ROW_CHUNKS
+    late = (PAIRS - EARLY) * 4
     right = jnp.transpose(right_block, (1, 0, 2))
     vmem = pl.BlockSpec(memory_space=pltpu.VMEM)
     hbm = pl.BlockSpec(memory_space=pltpu.HBM)
@@ -396,7 +396,7 @@
         in_specs=[vmem, vmem, vmem],
         out_specs=pl.BlockSpec(memory_space=pl.ANY),
         scratch_shapes=[
-            pltpu.VMEM((late, rows, width), jnp.float32),
+            pltpu.VMEM((late, rows_all // 2, width // 2), jnp.float32),
             pltpu.SemaphoreType.DMA((late + 1,)),
         ],
         compiler_params=pltpu.CompilerParams(vmem_limit_bytes=20 << 20),

time: 55.8 us -> 51.5 us (0.923)
  Pallas kernels: 54.4 us -> 50.3 us
    pallas_call x1, Pallas kernels: 48.3 us -> 44.2 us  [per_device(): pl.pallas_call(gather_kernel, out_shape=(pltpu.VMEM((ROW_CHUNKS, 2 * rows...]
where the time goes in v6:
time: 51.5 us; the launch traced here: 51.4 us
  Pallas kernels  50.3 us (98%)
  local copies, waits for them, and re-layouts  1.1 us (2%)
    pallas_call x1, Pallas kernels, per_device(): pl.pallas_call(gather_kernel, out_shape=(pltpu.VMEM((ROW_CHUNKS, 2 * rows...  44.2 us
    pallas_call x1, Pallas kernels, per_device(): pl.pallas_call(finish_kernel, out_shape=jax.ShapeDtypeStruct((rows_all, c...  6.1 us
    unnamed x1, local copies, waits for them, and re-layouts  1.1 us

profile of v6, /device:TPU:1, one launch (start us, length us, event | category | flops | bytes accessed | tf_op | source)
XLA Modules:
  0.0 51.4 jit_solution(13142872774076920402)
XLA Ops:
  0.0 1.1 %copy.7 = bf16[16,2,4096]{2,0,1:T(8,128)(2,1)S(1)} copy(bf16[16,2,4096]{2,1,0:T(2,128)(2,1)} %param.5) | data formatting | bytes 524288 | tf_op args[1]
  1.1 44.2 %shard_map.46 = (bf16[4,512,1024]{2,1,0:T(8,128)(2,1)S(1)}, bf16[4,2,2,2,4,4,16,512]{7,6,5,4,3,2,1,0:T(8,128)(2,1)S(1)}, f32[1024,3072]{1,0:T(8,128)S(1)}) custom-call(s32[4]{0:T(128)} %ids_hbm.1, s32[9]{0:T(128)} %order_hbm.1, bf16[4,1024,128]{2,1,0:T(8,128)(2,1)} %left_hbm.1, bf16[2,16,4096]{2,1,0:T(8,128)(2,1)S(1)} %bitcast.3), custom_call_target="tpu_custom_call" | custom-call | tf_op jit(solution)/shard_map/pallas_call | solution.py:369
  45.3 6.1 %shard_map.47 = f32[1024,4096]{1,0:T(8,128)} custom-call(bf16[4,512,1024]{2,1,0:T(8,128)(2,1)S(1)} %get-tuple-element.8.a_ref, bf16[4,2,2,2,4,4,16,512]{7,6,5,4,3,2,1,0:T(8,128)(2,1)S(1)} %get-tuple-element.9.b_ref, f32[1024,3072]{1,0:T(8,128)S(1)} %get-tuple-element.10.part_ref), custom_call_target="tpu_custom_call" | custom-call | tf_op jit(solution)/shard_map/pallas_call | solution.py:393

commit v7 on v6

--- a/solution.py
+++ b/solution.py
@@ -301,15 +301,15 @@
     tile(0, 0, 1)
     group_last(1)
     left_whole(2)
+    left_whole(3)
+    tile(1, 0, 0)
+    group_forward(3)
+    tile(1, 0, 1)
     whole(1, 0)
     tile(0, 1, 0)
+    group_last(2)
     whole(1, 1)
-    group_forward(3)
     tile(0, 1, 1)
-    left_whole(3)
-    tile(1, 0, 0)
-    tile(1, 0, 1)
-    group_last(2)
     tile(1, 1, 0)
     group_last(3)
     tile(1, 1, 1)

time: 51.5 us -> 50.2 us (0.975)
  Pallas kernels: 50.3 us -> 49 us
    pallas_call x1, Pallas kernels: 44.2 us -> 42.9 us  [per_device(): pl.pallas_call(gather_kernel, out_shape=(pltpu.VMEM((ROW_CHUNKS, 2 * rows...]
where the time goes in v7:
time: 50.2 us; the launch traced here: 50.1 us
  Pallas kernels  49 us (98%)
  local copies, waits for them, and re-layouts  1.1 us (2%)
    pallas_call x1, Pallas kernels, per_device(): pl.pallas_call(gather_kernel, out_shape=(pltpu.VMEM((ROW_CHUNKS, 2 * rows...  42.9 us
    pallas_call x1, Pallas kernels, per_device(): pl.pallas_call(finish_kernel, out_shape=jax.ShapeDtypeStruct((rows_all, c...  6.1 us
    unnamed x1, local copies, waits for them, and re-layouts  1.1 us

profile of v7, /device:TPU:1, one launch (start us, length us, event | category | flops | bytes accessed | tf_op | source)
XLA Modules:
  0.0 50.1 jit_solution(12125852149034546442)
XLA Ops:
  0.0 1.1 %copy.7 = bf16[16,2,4096]{2,0,1:T(8,128)(2,1)S(1)} copy(bf16[16,2,4096]{2,1,0:T(2,128)(2,1)} %param.5) | data formatting | bytes 524288 | tf_op args[1]
  1.1 42.9 %shard_map.46 = (bf16[4,512,1024]{2,1,0:T(8,128)(2,1)S(1)}, bf16[4,2,2,2,4,4,16,512]{7,6,5,4,3,2,1,0:T(8,128)(2,1)S(1)}, f32[1024,3072]{1,0:T(8,128)S(1)}) custom-call(s32[4]{0:T(128)} %ids_hbm.1, s32[9]{0:T(128)} %order_hbm.1, bf16[4,1024,128]{2,1,0:T(8,128)(2,1)} %left_hbm.1, bf16[2,16,4096]{2,1,0:T(8,128)(2,1)S(1)} %bitcast.3), custom_call_target="tpu_custom_call" | custom-call | tf_op jit(solution)/shard_map/pallas_call | solution.py:369
  44.0 6.1 %shard_map.47 = f32[1024,4096]{1,0:T(8,128)} custom-call(bf16[4,512,1024]{2,1,0:T(8,128)(2,1)S(1)} %get-tuple-element.8.a_ref, bf16[4,2,2,2,4,4,16,512]{7,6,5,4,3,2,1,0:T(8,128)(2,1)S(1)} %get-tuple-element.9.b_ref, f32[1024,3072]{1,0:T(8,128)S(1)} %get-tuple-element.10.part_ref), custom_call_target="tpu_custom_call" | custom-call | tf_op jit(solution)/shard_map/pallas_call | solution.py:393

commit v8 on v7

--- a/solution.py
+++ b/solution.py
@@ -33,13 +33,14 @@
     ids_hbm,
     order_hbm,
     left_hbm,
-    right_ref,
+    right_hbm,
     a_ref,
     b_ref,
     part_ref,
     ids,
     order,
     left,
+    right,
     code,
     pick,
     local,
@@ -48,7 +49,7 @@
     left_recv,
 ):
     slices, rows_all, part_k = left.shape
-    values, shard_k, columns = right_ref.shape
+    shard_k, values, columns = right.shape
     rows, width = rows_all // ROW_CHUNKS, columns // PAIRS
     strip = width // 2
     bond = 4 * part_k
@@ -76,6 +77,8 @@
     for other in (along_y(1), along_y(3), along_z(1), along_z(3), along_x(1), along_x(3), sibling):
         pl.semaphore_signal(barrier, inc=1, device_id=other, device_id_type=MESH)
 
+    shard = pltpu.make_async_copy(right_hbm, right, local.at[3])
+    shard.start()
     staged = [
         pltpu.make_async_copy(left_hbm, left, local.at[0]),
         pltpu.make_async_copy(ids_hbm, ids, local.at[1]),
@@ -83,10 +86,12 @@
     ]
     for one in staged:
         one.start()
+    shard.wait()
     for p in range(PAIRS):
         for half in (0, 1):
             at = p * width + half * strip
-            b_ref[p, half, :, core, z, y] = right_ref[:, :, at : at + strip]
+            for v in range(values):
+                b_ref[p, half, v, core, z, y] = right[:, v, at : at + strip]
 
     def copy(ref, signals, device):
         return pltpu.make_async_remote_copy(
@@ -210,8 +215,8 @@
     place_at = lax.broadcasted_iota(jnp.int32, (8, bond), 1)
     j = place_at & 15
     at_y, at_z, plane = (place_at >> 4) & 3, (place_at >> 6) & 3, place_at >> 8
-    shard = at_z * 8 + (at_y >> 1) * 4 + plane * 2 + (at_y & 1)
-    logical = shard * shard_k + j
+    origin = at_z * 8 + (at_y >> 1) * 4 + plane * 2 + (at_y & 1)
+    logical = origin * shard_k + j
     stored = jnp.zeros((8, bond), jnp.int32)
     for bit in range(order.shape[0]):
         stored = stored + ((logical >> bit) & 1) * jnp.left_shift(jnp.int32(1), order[bit])
@@ -363,7 +368,6 @@
     rows, width = rows_all // ROW_CHUNKS, columns // PAIRS
     bond = 4 * part_k
     late = (PAIRS - EARLY) * 4
-    right = jnp.transpose(right_block, (1, 0, 2))
     vmem = pl.BlockSpec(memory_space=pltpu.VMEM)
     hbm = pl.BlockSpec(memory_space=pltpu.HBM)
     a, b, part = pl.pallas_call(
@@ -373,15 +377,16 @@
             pltpu.VMEM((PAIRS, 2, values, 2, 4, 4, shard_k, width // 2), jnp.bfloat16),
             pltpu.VMEM((rows_all, EARLY * width), jnp.float32),
         ),
-        in_specs=[hbm, hbm, hbm, vmem],
+        in_specs=[hbm, hbm, hbm, hbm],
         out_specs=(vmem, vmem, vmem),
         scratch_shapes=[
             pltpu.SMEM(slice_ids.shape, jnp.int32),
             pltpu.SMEM(mode_order.shape, jnp.int32),
             pltpu.VMEM(left_block.shape, left_block.dtype),
+            pltpu.VMEM(right_block.shape, right_block.dtype),
             pltpu.VMEM((ROW_CHUNKS, 4, values, rows + 16, part_k), jnp.int16),
             pltpu.VMEM((bond, bond), jnp.bfloat16),
-            pltpu.SemaphoreType.DMA((3,)),
+            pltpu.SemaphoreType.DMA((4,)),
             pltpu.SemaphoreType.DMA((7,)),
             pltpu.SemaphoreType.DMA((2, 9, PAIRS)),
             pltpu.SemaphoreType.DMA((4, ROW_CHUNKS)),
@@ -389,7 +394,7 @@
         compiler_params=pltpu.CompilerParams(
             collective_id=0, has_side_effects=True, vmem_limit_bytes=20 << 20
         ),
-    )(*(pltpu.with_memory_space_constraint(x, pltpu.HBM) for x in (slice_ids, mode_order, left_block)), right)
+    )(*(pltpu.with_memory_space_constraint(x, pltpu.HBM) for x in (slice_ids, mode_order, left_block, right_block)))
     return pl.pallas_call(
         finish_kernel,
         out_shape=jax.ShapeDtypeStruct((rows_all, columns), jnp.float32),

time: 50.2 us -> 49 us (0.976)
  local copies, waits for them, and re-layouts: 1.1 us -> 0 us
    unnamed x1 -> x0, local copies, waits for them, and re-layouts: 1.1 us -> none
where the time goes in v8:
time: 49 us; the launch traced here: 48.8 us
  Pallas kernels  48.8 us (100%)
    pallas_call x1, Pallas kernels, per_device(): pl.pallas_call(gather_kernel, out_shape=(pltpu.VMEM((ROW_CHUNKS, 2 * rows...  42.7 us
    pallas_call x1, Pallas kernels, per_device(): pl.pallas_call(finish_kernel, out_shape=jax.ShapeDtypeStruct((rows_all, c...  6.1 us

profile of v8, /device:TPU:1, one launch (start us, length us, event | category | flops | bytes accessed | tf_op | source)
XLA Modules:
  0.0 48.8 jit_solution(10493376319996612858)
XLA Ops:
  0.0 42.7 %shard_map.46 = (bf16[4,512,1024]{2,1,0:T(8,128)(2,1)S(1)}, bf16[4,2,2,2,4,4,16,512]{7,6,5,4,3,2,1,0:T(8,128)(2,1)S(1)}, f32[1024,3072]{1,0:T(8,128)S(1)}) custom-call(s32[4]{0:T(128)} %ids_hbm.1, s32[9]{0:T(128)} %order_hbm.1, bf16[4,1024,128]{2,1,0:T(8,128)(2,1)} %left_hbm.1, bf16[16,2,4096]{2,1,0:T(2,128)(2,1)} %right_hbm.1), custom_call_target="tpu_custom_call" | custom-call | tf_op jit(solution)/shard_map/pallas_call | solution.py:373
  42.7 6.1 %shard_map.47 = f32[1024,4096]{1,0:T(8,128)} custom-call(bf16[4,512,1024]{2,1,0:T(8,128)(2,1)S(1)} %get-tuple-element.8.a_ref, bf16[4,2,2,2,4,4,16,512]{7,6,5,4,3,2,1,0:T(8,128)(2,1)S(1)} %get-tuple-element.9.b_ref, f32[1024,3072]{1,0:T(8,128)S(1)} %get-tuple-element.10.part_ref), custom_call_target="tpu_custom_call" | custom-call | tf_op jit(solution)/shard_map/pallas_call | solution.py:398

commit v9 on v8

--- a/solution.py
+++ b/solution.py
@@ -12,7 +12,7 @@
 ROW_CHUNKS = 4
 PAIRS = 4
 AHEAD = 1
-EARLY = 3
+EARLY = 5
 CODE_TOP = 32000.0
 STEPS_PER_OCTAVE = 16.0
 LN2 = math.log(2.0)
@@ -307,10 +307,10 @@
     group_last(1)
     left_whole(2)
     left_whole(3)
+    group_forward(3)
     tile(1, 0, 0)
-    group_forward(3)
+    whole(1, 0)
     tile(1, 0, 1)
-    whole(1, 0)
     tile(0, 1, 0)
     group_last(2)
     whole(1, 1)
@@ -318,10 +318,10 @@
     tile(1, 1, 0)
     group_last(3)
     tile(1, 1, 1)
-    for half in (0, 1):
-        whole(2, half)
-        tile(0, 2, half)
-        tile(1, 2, half)
+    whole(2, 0)
+    tile(0, 2, 0)
+    tile(1, 2, 0)
+    whole(2, 1)
     whole(3, 0)
     whole(3, 1)
 
@@ -345,11 +345,11 @@
 
     def out_copy(n):
         here = pl.ds(pl.multiple_of(n % 2 * rows, rows), rows)
-        cols = pl.ds(pl.multiple_of((n // 2 + 2 * EARLY) * width, width), width)
+        cols = pl.ds(pl.multiple_of((n // 2 + EARLY) * width, width), width)
         return pltpu.make_async_copy(last.at[n], out_ref.at[here, cols], sems.at[n])
 
     def one(n, carry):
-        last[n] = tile_product(a_ref, b_ref, n % 2, n // 4 + EARLY, n // 2 % 2)
+        last[n] = tile_product(a_ref, b_ref, n % 2, (n // 2 + EARLY) // 2, (n // 2 + EARLY) % 2)
         out_copy(n).start()
         return carry
 
@@ -367,7 +367,7 @@
     shard_k, values, columns = right_block.shape
     rows, width = rows_all // ROW_CHUNKS, columns // PAIRS
     bond = 4 * part_k
-    late = (PAIRS - EARLY) * 4
+    late = (2 * PAIRS - EARLY) * 2
     vmem = pl.BlockSpec(memory_space=pltpu.VMEM)
     hbm = pl.BlockSpec(memory_space=pltpu.HBM)
     a, b, part = pl.pallas_call(
@@ -375,7 +375,7 @@
         out_shape=(
             pltpu.VMEM((ROW_CHUNKS, 2 * rows, values * bond), jnp.bfloat16),
             pltpu.VMEM((PAIRS, 2, values, 2, 4, 4, shard_k, width // 2), jnp.bfloat16),
-            pltpu.VMEM((rows_all, EARLY * width), jnp.float32),
+            pltpu.VMEM((rows_all, EARLY * width // 2), jnp.float32),
         ),
         in_specs=[hbm, hbm, hbm, hbm],
         out_specs=(vmem, vmem, vmem),

time: 49 us -> 49.1 us (level)
    pallas_call x1, Pallas kernels: 6.1 us -> 8.55 us  [per_device(): pl.pallas_call(finish_kernel, out_shape=jax.ShapeDtypeStruct((rows_all, c...]
    pallas_call x1, Pallas kernels: 42.7 us -> 40.4 us  [per_device(): pl.pallas_call(gather_kernel, out_shape=(pltpu.VMEM((ROW_CHUNKS, 2 * rows...]
where the time goes in v9:
time: 49.1 us; the launch traced here: 49 us
  Pallas kernels  49 us (100%)
    pallas_call x1, Pallas kernels, per_device(): pl.pallas_call(gather_kernel, out_shape=(pltpu.VMEM((ROW_CHUNKS, 2 * rows...  40.4 us
    pallas_call x1, Pallas kernels, per_device(): pl.pallas_call(finish_kernel, out_shape=jax.ShapeDtypeStruct((rows_all, c...  8.55 us

profile of v9, /device:TPU:1, one launch (start us, length us, event | category | flops | bytes accessed | tf_op | source)
XLA Modules:
  0.0 49.0 jit_solution(13688528986141358185)
XLA Ops:
  0.0 40.4 %shard_map.46 = (bf16[4,512,1024]{2,1,0:T(8,128)(2,1)S(1)}, bf16[4,2,2,2,4,4,16,512]{7,6,5,4,3,2,1,0:T(8,128)(2,1)S(1)}, f32[1024,2560]{1,0:T(8,128)S(1)}) custom-call(s32[4]{0:T(128)} %ids_hbm.1, s32[9]{0:T(128)} %order_hbm.1, bf16[4,1024,128]{2,1,0:T(8,128)(2,1)} %left_hbm.1, bf16[16,2,4096]{2,1,0:T(2,128)(2,1)} %right_hbm.1), custom_call_target="tpu_custom_call" | custom-call | tf_op jit(solution)/shard_map/pallas_call | solution.py:373
  40.4 8.6 %shard_map.47 = f32[1024,4096]{1,0:T(8,128)} custom-call(bf16[4,512,1024]{2,1,0:T(8,128)(2,1)S(1)} %get-tuple-element.8.a_ref, bf16[4,2,2,2,4,4,16,512]{7,6,5,4,3,2,1,0:T(8,128)(2,1)S(1)} %get-tuple-element.9.b_ref, f32[1024,2560]{1,0:T(8,128)S(1)} %get-tuple-element.10.part_ref), custom_call_target="tpu_custom_call" | custom-call | tf_op jit(solution)/shard_map/pallas_call | solution.py:398
